TPU v7x, 128 devices: a whole 4x4x4 slice. The times are simulated.
128 devices in a mesh: req: 8 (over y, core), row: 4 (over z), col: 4 (over x).
Axes of the slice: x: 4, y: 4, z: 4, core: 2. Of those that a mesh axis runs over, the one named last changes fastest.
Arguments:
- tokens: bfloat16 [16384, 1024], P(('req', 'row')), may hold values from -6 to 6
- norm_gain: float32 [1024], replicated, may hold values from 0.5 to 1.5
- w_attn: bfloat16 [5, 1024, 1024], P(None, 'row', 'col'), may hold values from -1 to 1
- persist_kv: bfloat16 [2, 16, 1024], P(None, None, 'col'), may hold values from -6 to 6
- kv_pool: bfloat16 [32, 32, 1, 256, 2, 1024], P(('req', 'row'), None, None, None, None, 'col'), may hold values from -6 to 6
- cache_len: int32 [32], replicated, may hold values from 0 to 8192, as said below
- mem_state: float32 [32, 8, 128, 128], P(('req', 'row'), 'col'), may hold values from -0.5 to 0.5
- decay: float32 [32, 8, 8], P(('req', 'row'), None, 'col'), may hold values from 0.6 to 1
- rate: float32 [32, 8, 8], P(('req', 'row'), None, 'col'), may hold values from 0.05 to 0.5
Outputs:
- mixed: bfloat16 [16384, 1024], P(('req', 'row'), 'col')
- new_state: float32 [32, 8, 128, 128], P(('req', 'row'), 'col')
Inputs may be any that keep to these rules, and one draw needn't show every extreme that they name: `cache_len`: cached tokens before each block; some block has exactly 8192.
All inputs are finite; a program needn't handle non-finite values.
Results may differ from a plain program's by a relative error of at most 0.006.
Values may be sent and summed in bfloat16 or wider, within the bound.
A program may use at most 192 MiB of HBM per device.

v0:
```python
import jax
import jax.numpy as jnp
from jax import lax
from jax.sharding import PartitionSpec as P

HD = 128
NP = 16
SEG = 64
negative_fill = -1e30


def attend(query_heads, key_heads, value_heads, allowed):
    scores = jnp.einsum(
        "...shd,...khd->...hsk", query_heads, key_heads, preferred_element_type=jnp.float32
    ) * query_heads.shape[-1] ** (-0.5)
    allowed = allowed[..., None, :, :]
    scores = jnp.where(allowed, scores, negative_fill)
    maxima = jnp.max(scores, axis=-1)
    probabilities = jnp.where(allowed, jnp.exp(scores - maxima[..., None]), 0.0)
    totals = jnp.sum(probabilities, axis=-1)
    weighted = jnp.einsum(
        "...hsk,...khd->...shd",
        probabilities.astype(jnp.bfloat16),
        value_heads,
        preferred_element_type=jnp.float32,
    )
    return (weighted, jnp.swapaxes(maxima, -1, -2), jnp.swapaxes(totals, -1, -2))


def combine_parts(first_part, second_part):
    output_a, maxima_a, totals_a = first_part
    output_b, maxima_b, totals_b = second_part
    highest = jnp.maximum(maxima_a, maxima_b)
    factor_a = jnp.exp(maxima_a - highest)
    factor_b = jnp.exp(maxima_b - highest)
    merged = output_a * factor_a[..., None] + output_b * factor_b[..., None]
    return (merged, highest, totals_a * factor_a + totals_b * factor_b)


def shards(tokens, norm_gain, w_attn, persist_kv, kv_pool, cache_len, mem_state, decay, rate):
    pool_size = lax.axis_size(("req", "row"))
    my_index = lax.axis_index(("req", "row"))
    column = lax.axis_index("col")
    length = tokens.shape[0]
    local_width = w_attn.shape[2]
    heads_here = local_width // HD
    xfloat = tokens.astype(jnp.float32)
    normed = (
        xfloat * lax.rsqrt(jnp.mean(xfloat * xfloat, axis=-1, keepdims=True) + 1e-05) * norm_gain
    ).astype(jnp.bfloat16)
    gathered = lax.all_gather(w_attn, "row", axis=1, tiled=True)
    projected = jnp.einsum("sd,wdc->wsc", normed, gathered[:4], preferred_element_type=jnp.float32)
    queries = projected[0].astype(jnp.bfloat16).reshape(length, heads_here, HD)
    keys_own = projected[1].astype(jnp.bfloat16).reshape(length, heads_here, HD)
    values_own = projected[2].astype(jnp.bfloat16).reshape(length, heads_here, HD)
    gate_open = jax.nn.sigmoid(projected[3]).reshape(length, heads_here, HD)
    persist = persist_kv.reshape(2, NP, heads_here, HD)
    keys_cat = jnp.concatenate([persist[0], keys_own], axis=0)
    vals_cat = jnp.concatenate([persist[1], values_own], axis=0)
    positions = jnp.arange(length, dtype=jnp.int32)
    causal = positions[:, None] >= positions[None, :]
    allowed = jnp.concatenate([jnp.ones((length, NP), dtype=bool), causal], axis=1)
    local_part = attend(queries, keys_cat, vals_cat, allowed)
    page_pool = kv_pool[0]
    slot_count = page_pool.shape[1]
    page_len = page_pool.shape[2]
    slot_ids = jnp.arange(slot_count, dtype=jnp.int32)[None, :, None]
    offsets = jnp.arange(page_len, dtype=jnp.int32)[None, None, :]
    peer_ids = jnp.arange(pool_size, dtype=jnp.int32)[:, None, None]
    everyone = lax.all_gather(queries[None], ("req", "row"), axis=0, tiled=True)
    page_ids = slot_ids * pool_size + (my_index - peer_ids) % pool_size
    places = (page_ids * page_len + offsets).reshape(pool_size, slot_count * page_len)
    usable = (places < cache_len[:, None])[:, None, :]
    cache_keys = page_pool[:, :, :, 0].reshape(pool_size, slot_count * page_len, heads_here, HD)
    cache_vals = page_pool[:, :, :, 1].reshape(pool_size, slot_count * page_len, heads_here, HD)
    part_out, part_max, part_tot = attend(everyone, cache_keys, cache_vals, usable)
    got_out, got_max, got_tot = (
        lax.all_to_all(part_out, ("req", "row"), split_axis=0, concat_axis=0, tiled=True),
        lax.all_to_all(part_max, ("req", "row"), split_axis=0, concat_axis=0, tiled=True),
        lax.all_to_all(part_tot, ("req", "row"), split_axis=0, concat_axis=0, tiled=True),
    )
    highest = jnp.max(got_max, axis=0)
    scaling = jnp.exp(got_max - highest[None])
    cache_part = (
        jnp.sum(got_out * scaling[..., None], axis=0),
        highest,
        jnp.sum(got_tot * scaling, axis=0),
    )
    total_part = combine_parts(local_part, cache_part)
    attended = total_part[0] / total_part[2][..., None]
    query_float = queries.astype(jnp.float32)
    key_float = keys_own.astype(jnp.float32)
    value_float = values_own.astype(jnp.float32)
    query_unit = query_float * lax.rsqrt(
        jnp.sum(query_float * query_float, axis=-1, keepdims=True) + 1e-06
    )
    key_unit = key_float * lax.rsqrt(jnp.sum(key_float * key_float, axis=-1, keepdims=True) + 1e-06)
    memory = mem_state[0]
    outputs = []
    for segment in range(length // SEG):
        lower = segment * SEG
        seg_query = query_unit[lower : lower + SEG]
        seg_keys = key_unit[lower : lower + SEG]
        seg_values = value_float[lower : lower + SEG]
        outputs.append(
            jnp.einsum("shd,hde->she", seg_query, memory, precision=lax.Precision.HIGHEST)
        )
        errors = (
            jnp.einsum("shd,hde->she", seg_keys, memory, precision=lax.Precision.HIGHEST)
            - seg_values
        )
        update = jnp.einsum("shd,she->hde", seg_keys, errors, precision=lax.Precision.HIGHEST)
        memory = (
            decay[0, segment][:, None, None] * memory - rate[0, segment][:, None, None] * update
        )
    recalled = jnp.concatenate(outputs, axis=0)
    combined = (attended + gate_open * recalled).reshape(length, local_width).astype(jnp.bfloat16)
    output_terms = lax.dot_general(
        combined, gathered[4], (((1,), (1,)), ((), ())), preferred_element_type=jnp.float32
    )
    summed = lax.psum_scatter(
        output_terms.astype(jnp.bfloat16), "col", scatter_dimension=1, tiled=True
    ).astype(jnp.float32)
    own_cols = lax.dynamic_slice_in_dim(xfloat, column * summed.shape[1], summed.shape[1], 1)
    mixed = (own_cols + summed).astype(jnp.bfloat16)
    return (mixed, memory[None])


def solution(mesh):
    return jax.shard_map(
        shards,
        mesh=mesh,
        in_specs=(
            P(("req", "row"), None),
            P(),
            P(None, "row", "col"),
            P(None, None, "col"),
            P(("req", "row"), None, None, None, None, "col"),
            P(),
            P(("req", "row"), "col", None, None),
            P(("req", "row"), None, "col"),
            P(("req", "row"), None, "col"),
        ),
        out_specs=(P(("req", "row"), "col"), P(("req", "row"), "col", None, None)),
        check_vma=False,
    )
```

profile of v0, /device:TPU:0, one launch (start us, length us, event | category | flops | bytes accessed | tf_op | source)
XLA Modules:
  0.0 469.1 jit_solution(4142681741803543050)
XLA Ops:
  7.2 2.2 copy.50
  9.4 1.5 multiply_reduce_fusion.1
  11.0 39.7 %all-gather.3.cloned.1.call-done = bf16[5,1024,256]{1,2,0:T(8,128)(2,1)} async-done(((bf16[5,256,256]{1,2,0:T(8,128)(2,1)}), bf16[5,1024,256]{1,2,0:T(8,128)(2,1)}) %all-gather.3.cloned.1.call-update) | async-done | bytes 2621456 | tf_op jit(solution)/shard_map/all_gather | solution.py:51
  50.7 3.3 fusion.109
  54.0 1.4 copy-done.9
  56.3 20.9 %copy.57 = bf16[1,32,1,256,2,256]{3,5,1,4,2,0:T(8,128)(2,1)} copy(bf16[1,32,1,256,2,256]{5,4,3,2,1,0:T(2,128)(2,1)} %param.13) | data formatting | bytes 16777216 | tf_op args[4]
  77.3 6.0 %fusion.106 = (bf16[32,1,256,1,256]{2,4,0,3,1:T(8,128)(2,1)}, bf16[32,1,256,1,256]{2,4,0,3,1:T(8,128)(2,1)}) fusion(bf16[32,1,256,2,256]{2,4,0,3,1:T(8,128)(2,1)} %bitcast.129), kind=kLoop, calls=%fused_computation.168 | loop fusion | bytes 16777216 | tf_op jit(solution)/shard_map/slice | solution.py:74
  83.3 26.7 %all-gather.5.cloned.1.call-done = bf16[32,512,2,128]{3,1,2,0:T(8,128)(2,1)} async-done(((bf16[1,512,2,128]{3,1,2,0:T(8,128)(2,1)}), bf16[32,512,2,128]{3,1,2,0:T(8,128)(2,1)}) %all-gather.5.cloned.1.call-update) | async-done | bytes 8388624 | tf_op jit(solution)/shard_map/all_gather | solution.py:70
  110.1 18.0 %fusion = (f32[32,2,512]{2,1,0:T(2,128)}, f32[32,2,512,256]{2,3,1,0:T(8,128)}) fusion(pred[32,256]{1,0:T(8,128)(4,1)S(1)} %add_compare_fusion, bf16[32,512,2,128]{3,1,2,0:T(8,128)(2,1)} %all-gather.5.cloned.1.call-done, bf16[32,256,2,128]{1,3,2,0:T(8,128)(2,1)} %bitcast.130), kind=kOutput, calls=%fused_computation.2 | convolution fusion | flops 2172616704 | bytes 46276608 | tf_op jit(solution)/shard_map/...shd,...khd->...hsk/dot_general | solution.py:13
  128.1 5.5 %all-to-all-start = ((f32[32,512,2]{1,2,0:T(2,128)}), f32[32,512,2]{1,2,0:T(2,128)S(1)}, u32[]{:S(2)}, u32[]{:S(2)}) async-start(f32[32,512,2]{1,2,0:T(2,128)} %bitcast.10), calls=%async_computation | async-start | bytes 262144 | tf_op jit(solution)/shard_map/all_to_all | solution.py:79
  133.6 16.1 %fusion.1 = f32[32,2,512]{2,1,0:T(2,128)} fusion(f32[32,2,512,256]{2,3,1,0:T(8,128)} %get-tuple-element.34, f32[32,2,512]{2,1,0:T(2,128)} %get-tuple-element.33, pred[32,256]{1,0:T(8,128)(4,1)S(1)} %add_compare_fusion), kind=kLoop, calls=%fused_computation.3 | loop fusion | flops 41910272 | bytes 33824768 | tf_op jit(solution)/shard_map/reduce_sum | solution.py:20
  149.6 7.6 %all-to-all-start.2 = ((f32[32,512,2]{1,2,0:T(2,128)}), f32[32,512,2]{1,2,0:T(2,128)S(1)}, u32[]{:S(2)}, u32[]{:S(2)}) async-start(f32[32,512,2]{1,2,0:T(2,128)} %bitcast.14), calls=%async_computation.2 | async-start | bytes 262144 | tf_op jit(solution)/shard_map/all_to_all | solution.py:80
  157.2 22.5 %fusion.10 = f32[32,512,2,128]{3,1,2,0:T(8,128)} fusion(bf16[32,256,2,128]{1,3,2,0:T(8,128)(2,1)} %bitcast.131, f32[32,2,512,256]{2,3,1,0:T(8,128)} %get-tuple-element.34, f32[32,2,512]{2,1,0:T(2,128)} %get-tuple-element.33, pred[32,256]{1,0:T(8,128)(4,1)S(1)} %add_compare_fusion), kind=kOutput, calls=%fused_computation.12 | convolution fusion | flops 2189426688 | bytes 54665216 | tf_op jit(solution)/shard_map/...hsk,...khd->...shd/dot_general | solution.py:21
  180.4 7.3 %all-to-all-start.1 = ((f32[32,512,2,128]{3,1,2,0:T(8,128)}), f32[32,512,2,128]{3,1,2,0:T(8,128)}, u32[]{:S(2)}, u32[]{:S(2)}) async-start(f32[32,512,2,128]{3,1,2,0:T(8,128)} %fusion.10), calls=%async_computation.1 | async-start | bytes 33554432 | tf_op jit(solution)/shard_map/all_to_all | solution.py:78
  193.0 1.2 convolution_bitcast_fusion.7
  194.2 1.2 fusion.27
  196.7 1.2 convolution_bitcast_fusion.6
  197.9 1.2 fusion.28
  200.3 1.2 convolution_bitcast_fusion.5
  201.5 1.2 fusion.29
  205.1 1.2 fusion.30
  208.8 1.2 fusion.31
  211.1 1.2 convolution_bitcast_fusion.2
  212.4 1.2 fusion.32
  215.9 2.0 fusion.57
  219.2 190.2 %all-to-all-done.1 = f32[32,512,2,128]{3,1,2,0:T(8,128)} async-done(((f32[32,512,2,128]{3,1,2,0:T(8,128)}), f32[32,512,2,128]{3,1,2,0:T(8,128)}, u32[]{:S(2)}, u32[]{:S(2)}) %all-to-all-start.1) | async-done | bytes 16777248 | tf_op jit(solution)/shard_map/all_to_all | solution.py:78
  409.4 7.6 %multiply_reduce_fusion = f32[512,2,128]{2,0,1:T(8,128)S(1)} fusion(f32[32,512,2,128]{3,1,2,0:T(8,128)} %all-to-all-done.1, f32[32,512,2]{1,2,0:T(2,128)S(1)} %get-tuple-element.22), kind=kLoop, calls=%fused_computation.6 | loop fusion | flops 8257536 | bytes 17432576 | tf_op jit(solution)/shard_map/reduce_sum | solution.py:85
  418.1 2.5 fusion.25
  420.6 2.5 convolution_convert_fusion
  424.5 1.9 fusion.34
  426.4 34.4 %reduce-scatter.2.cloned.1.call-done = bf16[512,256]{1,0:T(8,128)(2,1)} async-done(((bf16[512,1024]{1,0:T(8,128)(2,1)}), bf16[512,256]{1,0:T(8,128)(2,1)}) %reduce-scatter.2.cloned.1.call-update) | async-done | bytes 262160 | tf_op jit(solution)/shard_map/reduce_scatter | solution.py:121
  460.9 1.7 add_convert_fusion
  (80 shorter events, 20.9 us)
Async XLA Ops:
  7.2 43.5 %all-gather.3.cloned.1.call-start = ((), (), s32[]{:S(2)}) async-start(), calls=%async_computation.4 | async-start | bytes 3276800 | tf_op jit(solution)/shard_map/all_gather | solution.py:51
  9.4 100.7 %all-gather.5.cloned.1.call-start = ((), (), s32[]{:S(2)}) async-start(), calls=%async_computation.5 | async-start | bytes 8650752 | tf_op jit(solution)/shard_map/all_gather | solution.py:70
  54.0 1.4 copy-start.9
  56.3 21.0 %copy-start.13 = (s32[32]{0:T(128)S(1)}, s32[32]{0:T(128)}, u32[]{:S(2)}) copy-start(s32[32]{0:T(128)} %param.14) | copy-start | bytes 388
  128.1 21.6 %all-to-all-start = ((f32[32,512,2]{1,2,0:T(2,128)}), f32[32,512,2]{1,2,0:T(2,128)S(1)}, u32[]{:S(2)}, u32[]{:S(2)}) async-start(f32[32,512,2]{1,2,0:T(2,128)} %bitcast.10), calls=%async_computation | async-start | bytes 262144 | tf_op jit(solution)/shard_map/all_to_all | solution.py:79
  149.6 30.1 %all-to-all-start.2 = ((f32[32,512,2]{1,2,0:T(2,128)}), f32[32,512,2]{1,2,0:T(2,128)S(1)}, u32[]{:S(2)}, u32[]{:S(2)}) async-start(f32[32,512,2]{1,2,0:T(2,128)} %bitcast.14), calls=%async_computation.2 | async-start | bytes 262144 | tf_op jit(solution)/shard_map/all_to_all | solution.py:80
  179.7 8.1 %copy-start.12 = (bf16[2,16,256]{2,1,0:T(8,128)(2,1)S(1)}, bf16[2,16,256]{2,1,0:T(8,128)(2,1)}, u32[]{:S(2)}) copy-start(bf16[2,16,256]{2,1,0:T(8,128)(2,1)} %param.12) | copy-start | bytes 49156
  179.7 9.0 %copy-start.10 = (f32[1,8,2]{1,2,0:T(2,128)S(1)}, f32[1,8,2]{1,2,0:T(2,128)}, u32[]{:S(2)}) copy-start(f32[1,8,2]{1,2,0:T(2,128)} %param.17) | copy-start | bytes 196
  179.7 9.0 %copy-start.11 = (f32[1,8,2]{1,2,0:T(2,128)S(1)}, f32[1,8,2]{1,2,0:T(2,128)}, u32[]{:S(2)}) copy-start(f32[1,8,2]{1,2,0:T(2,128)} %param.16) | copy-start | bytes 196
  179.7 0.7 copy-start.7
  180.4 229.0 %all-to-all-start.1 = ((f32[32,512,2,128]{3,1,2,0:T(8,128)}), f32[32,512,2,128]{3,1,2,0:T(8,128)}, u32[]{:S(2)}, u32[]{:S(2)}) async-start(f32[32,512,2,128]{3,1,2,0:T(8,128)} %fusion.10), calls=%async_computation.1 | async-start | bytes 33554432 | tf_op jit(solution)/shard_map/all_to_all | solution.py:78
  187.7 2.7 copy-start.4
  187.7 273.1 %reduce-scatter.2.cloned.1.call-start = ((), (), s32[]{:S(2)}) async-start(), calls=%async_computation.6 | async-start | bytes 1310720 | tf_op jit(solution)/shard_map/reduce_scatter | solution.py:121
  189.3 1.1 copy-start.6
  189.8 2.0 copy-start.2
  190.5 2.5 copy-start.3
  191.1 0.8 copy-start
  195.5 22.4 %copy-start.5 = (pred[512,528]{0,1:T(8,128)(4,1)S(1)}, pred[512,528]{0,1:T(8,128)(4,1)}, u32[]{:S(2)}) copy-start(pred[512,528]{0,1:T(8,128)(4,1)} %concatenate.13) | copy-start | bytes 811012
  214.8 4.2 copy-start.8
  418.1 5.0 %copy-start.1 = (bf16[512,1024]{1,0:T(8,128)(2,1)S(1)}, bf16[512,1024]{1,0:T(8,128)(2,1)}, u32[]{:S(2)}) copy-start(bf16[512,1024]{1,0:T(8,128)(2,1)} %param.9) | copy-start | bytes 3145732
Sparse Core Ops, SparseCore 0:
  9.6 40.9 all-gather.2
  56.4 53.6 all-gather.4
  423.3 37.5 reduce-scatter.1
where the time goes:
time: 471 us; the launch traced here: 469 us
  waiting for transfers between devices  291 us (62%)
  matrix products  76.2 us (16%)
  local copies, waits for them, and re-layouts  36 us (8%)
  other arithmetic  31 us (7%)
  starting transfers between devices  20.5 us (4%)
  between operations  14.2 us (3%)
    all_to_all x1, waiting for transfers between devices, shards(): lax.all_to_all(part_out, ('req', 'row'), split_axis=0, concat_axis=0, til...  190 us
    all_gather x1, waiting for transfers between devices, shards(): gathered = lax.all_gather(w_attn, 'row', axis=1, tiled=True)  39.7 us
    reduce_scatter x1, waiting for transfers between devices, shards(): lax.psum_scatter(output_terms.astype(jnp.bfloat16), 'col', scatter_dimens...  34.4 us
    all_gather x1, waiting for transfers between devices, shards(): everyone = lax.all_gather(queries[None], ('req', 'row'), axis=0, tiled=True)  26.7 us
    unnamed x30, local copies, waits for them, and re-layouts  25.3 us
    dot_general x2, matrix products, attend(): jnp.einsum('...hsk,...khd->...shd', probabilities.astype(jnp.bfloat16), v...  25 us
    dot_general x2, matrix products, attend(): jnp.einsum('...shd,...khd->...hsk', query_heads, key_heads, preferred_ele...  18.5 us
    reduce_sum x2, other arithmetic, attend(): totals = jnp.sum(probabilities, axis=-1)  16.6 us
  transfers between devices with their start and end apart: 6, of which 4 were waited for; matrix products, arithmetic and copies ran while one was open for 22% of the time, Pallas kernels for 0%

commit v1 on v0

--- a/solution.py
+++ b/solution.py
@@ -2,6 +2,7 @@
 import jax.numpy as jnp
 from jax import lax
 from jax.sharding import PartitionSpec as P
+from jax.lax import axis_index, axis_size, ppermute
 
 HD = 128
 NP = 16
@@ -48,7 +49,27 @@
     normed = (
         xfloat * lax.rsqrt(jnp.mean(xfloat * xfloat, axis=-1, keepdims=True) + 1e-05) * norm_gain
     ).astype(jnp.bfloat16)
-    gathered = lax.all_gather(w_attn, "row", axis=1, tiled=True)
+    r1 = axis_size("row")
+    taken_in = axis_index("row")
+    seen_now, before, reached = (r1, taken_in, w_attn.shape[1])
+    samples = [(i, (i + 1) % seen_now) for i in range(seen_now)]
+    all_blocks = [(i, (i - 1) % seen_now) for i in range(seen_now)]
+    gathered = jnp.zeros(
+        (*w_attn.shape[:1], seen_now * reached, *w_attn.shape[1 + 1 :]), w_attn.dtype
+    )
+    gathered = lax.dynamic_update_slice_in_dim(gathered, w_attn, before * reached, axis=1)
+    e_now = block_out = w_attn
+    current_value = seen_now // 2
+    for c in range(1, current_value + 1):
+        e_now = ppermute(e_now, axis_name="row", perm=samples)
+        gathered = lax.dynamic_update_slice_in_dim(
+            gathered, e_now, (before - c) % seen_now * reached, axis=1
+        )
+        if c < seen_now - current_value:
+            block_out = ppermute(block_out, axis_name="row", perm=all_blocks)
+            gathered = lax.dynamic_update_slice_in_dim(
+                gathered, block_out, (before + c) % seen_now * reached, axis=1
+            )
     projected = jnp.einsum("sd,wdc->wsc", normed, gathered[:4], preferred_element_type=jnp.float32)
     queries = projected[0].astype(jnp.bfloat16).reshape(length, heads_here, HD)
     keys_own = projected[1].astype(jnp.bfloat16).reshape(length, heads_here, HD)

time: 471 us -> 462 us (0.981)
  waiting for transfers between devices: 291 us -> 271 us
    all_gather x1 -> x0, waiting for transfers between devices: 39.7 us -> none  [shards(): gathered = lax.all_gather(w_attn, 'row', axis=1, tiled=True)]
    ppermute x0 -> x3, waiting for transfers between devices: none -> 30.8 us  [the longest x2 30.8 us: shards(): e_now = ppermute(e_now, axis_name='row', perm=samples)]
    all_to_all x1, waiting for transfers between devices: 190 us -> 182 us  [shards(): lax.all_to_all(part_out, ('req', 'row'), split_axis=0, concat_axis=0, til...]
    unnamed x30 -> x52, local copies, waits for them, and re-layouts: 25.3 us -> 25.1 us
  transfers between devices with their start and end apart: 6 -> 8, of which waited for: 4 -> 5; matrix products, arithmetic and copies ran while one was open for 22% -> 24% of each run, Pallas kernels for 0% -> 0%
where the time goes in v1:
time: 462 us; the launch traced here: 460 us
  waiting for transfers between devices  271 us (59%)
  matrix products  80 us (17%)
  local copies, waits for them, and re-layouts  38.1 us (8%)
  other arithmetic  31.5 us (7%)
  starting transfers between devices  24.9 us (5%)
  between operations  14.7 us (3%)
    all_to_all x1, waiting for transfers between devices, shards(): lax.all_to_all(part_out, ('req', 'row'), split_axis=0, concat_axis=0, til...  182 us
    reduce_scatter x1, waiting for transfers between devices, shards(): lax.psum_scatter(output_terms.astype(jnp.bfloat16), 'col', scatter_dimens...  33 us
    ppermute x2, waiting for transfers between devices, shards(): e_now = ppermute(e_now, axis_name='row', perm=samples)  30.8 us
    unnamed x52, local copies, waits for them, and re-layouts  25.1 us
    dot_general x2, matrix products, attend(): jnp.einsum('...hsk,...khd->...shd', probabilities.astype(jnp.bfloat16), v...  25.1 us
    all_gather x1, waiting for transfers between devices, shards(): everyone = lax.all_gather(queries[None], ('req', 'row'), axis=0, tiled=True)  24.9 us
    dot_general x2, matrix products, attend(): jnp.einsum('...shd,...khd->...hsk', query_heads, key_heads, preferred_ele...  19.2 us
    reduce_sum x2, other arithmetic, attend(): totals = jnp.sum(probabilities, axis=-1)  16.6 us
  transfers between devices with their start and end apart: 8, of which 5 were waited for; matrix products, arithmetic and copies ran while one was open for 24% of the time, Pallas kernels for 0%

profile of v1, /device:TPU:0, one launch (start us, length us, event | category | flops | bytes accessed | tf_op | source)
XLA Modules:
  0.0 459.8 jit_solution(18041870960558107222)
XLA Ops:
  7.2 1.4 copy.54
  8.6 2.1 collective-permute-start
  10.7 2.2 collective-permute-start.1
  13.4 14.2 %collective-permute-done = bf16[5,256,256]{1,2,0:T(8,128)(2,1)S(1)} collective-permute-done((bf16[5,256,256]{1,2,0:T(8,128)(2,1)S(1)}, bf16[5,256,256]{1,2,0:T(8,128)(2,1)S(1)}, u32[]{:S(2)}, u32[]{:S(2)}) %collective-permute-start) | collective-permute-done | bytes 655392 | tf_op jit(solution)/shard_map/ppermute | solution.py:64
  28.1 16.6 %collective-permute-done.2 = bf16[5,256,256]{1,2,0:T(8,128)(2,1)S(1)} collective-permute-done((bf16[5,256,256]{1,2,0:T(8,128)(2,1)S(1)}, bf16[5,256,256]{1,2,0:T(8,128)(2,1)S(1)}, u32[]{:S(2)}, u32[]{:S(2)}) %collective-permute-start.2) | collective-permute-done | bytes 655392 | tf_op jit(solution)/shard_map/ppermute | solution.py:64
  44.8 2.3 fusion.104
  47.1 1.4 copy-done.8
  49.4 20.9 %copy.63 = bf16[1,32,1,256,2,256]{3,5,1,4,2,0:T(8,128)(2,1)} copy(bf16[1,32,1,256,2,256]{5,4,3,2,1,0:T(2,128)(2,1)} %param.13) | data formatting | bytes 16777216 | tf_op args[4]
  70.5 6.0 %fusion.101 = (bf16[32,1,256,1,256]{2,4,0,3,1:T(8,128)(2,1)}, bf16[32,1,256,1,256]{2,4,0,3,1:T(8,128)(2,1)}) fusion(bf16[32,1,256,2,256]{2,4,0,3,1:T(8,128)(2,1)} %bitcast.130), kind=kLoop, calls=%fused_computation.170 | loop fusion | bytes 16777216 | tf_op jit(solution)/shard_map/slice | solution.py:95
  76.4 24.9 %all-gather.2.cloned.1.call-done = bf16[32,512,2,128]{3,1,2,0:T(8,128)(2,1)} async-done(((bf16[1,512,2,128]{3,1,2,0:T(8,128)(2,1)}), bf16[32,512,2,128]{3,1,2,0:T(8,128)(2,1)}) %all-gather.2.cloned.1.call-update) | async-done | bytes 8388624 | tf_op jit(solution)/shard_map/all_gather | solution.py:91
  101.3 18.0 %fusion = (f32[32,2,512]{2,1,0:T(2,128)}, f32[32,2,512,256]{2,3,1,0:T(8,128)}) fusion(pred[32,256]{1,0:T(8,128)(4,1)S(1)} %add_compare_fusion, bf16[32,512,2,128]{3,1,2,0:T(8,128)(2,1)} %all-gather.2.cloned.1.call-done, bf16[32,256,2,128]{1,3,2,0:T(8,128)(2,1)} %bitcast.131), kind=kOutput, calls=%fused_computation.2 | convolution fusion | flops 2172616704 | bytes 46276608 | tf_op jit(solution)/shard_map/...shd,...khd->...hsk/dot_general | solution.py:14
  119.3 5.5 %all-to-all-start = ((f32[32,512,2]{1,2,0:T(2,128)}), f32[32,512,2]{1,2,0:T(2,128)S(1)}, u32[]{:S(2)}, u32[]{:S(2)}) async-start(f32[32,512,2]{1,2,0:T(2,128)} %bitcast.10), calls=%async_computation | async-start | bytes 262144 | tf_op jit(solution)/shard_map/all_to_all | solution.py:100
  124.8 16.1 %fusion.1 = f32[32,2,512]{2,1,0:T(2,128)} fusion(f32[32,2,512,256]{2,3,1,0:T(8,128)} %get-tuple-element.34, f32[32,2,512]{2,1,0:T(2,128)} %get-tuple-element.33, pred[32,256]{1,0:T(8,128)(4,1)S(1)} %add_compare_fusion), kind=kLoop, calls=%fused_computation.3 | loop fusion | flops 41910272 | bytes 33824768 | tf_op jit(solution)/shard_map/reduce_sum | solution.py:21
  140.9 7.6 %all-to-all-start.2 = ((f32[32,512,2]{1,2,0:T(2,128)}), f32[32,512,2]{1,2,0:T(2,128)S(1)}, u32[]{:S(2)}, u32[]{:S(2)}) async-start(f32[32,512,2]{1,2,0:T(2,128)} %bitcast.14), calls=%async_computation.2 | async-start | bytes 262144 | tf_op jit(solution)/shard_map/all_to_all | solution.py:101
  148.5 22.5 %fusion.10 = f32[32,512,2,128]{3,1,2,0:T(8,128)} fusion(bf16[32,256,2,128]{1,3,2,0:T(8,128)(2,1)} %bitcast.132, f32[32,2,512,256]{2,3,1,0:T(8,128)} %get-tuple-element.34, f32[32,2,512]{2,1,0:T(2,128)} %get-tuple-element.33, pred[32,256]{1,0:T(8,128)(4,1)S(1)} %add_compare_fusion), kind=kOutput, calls=%fused_computation.12 | convolution fusion | flops 2189426688 | bytes 54665216 | tf_op jit(solution)/shard_map/...hsk,...khd->...shd/dot_general | solution.py:22
  171.0 7.5 %all-to-all-start.1 = ((f32[32,512,2,128]{3,1,2,0:T(8,128)}), f32[32,512,2,128]{3,1,2,0:T(8,128)}, u32[]{:S(2)}, u32[]{:S(2)}) async-start(f32[32,512,2,128]{3,1,2,0:T(8,128)} %fusion.10), calls=%async_computation.1 | async-start | bytes 33554432 | tf_op jit(solution)/shard_map/all_to_all | solution.py:99
  190.7 1.3 convolution_bitcast_fusion.7
  198.0 1.9 convolution_bitcast_fusion.5
  202.3 1.9 convolution_bitcast_fusion.4
  206.6 1.9 convolution_bitcast_fusion.3
  209.7 1.9 convolution_bitcast_fusion.2
  211.6 1.4 concatenate.15
  213.0 2.0 fusion.52
  216.2 1.3 copy-done.3
  218.4 181.8 %all-to-all-done.1 = f32[32,512,2,128]{3,1,2,0:T(8,128)} async-done(((f32[32,512,2,128]{3,1,2,0:T(8,128)}), f32[32,512,2,128]{3,1,2,0:T(8,128)}, u32[]{:S(2)}, u32[]{:S(2)}) %all-to-all-start.1) | async-done | bytes 16777248 | tf_op jit(solution)/shard_map/all_to_all | solution.py:99
  400.2 7.8 %multiply_reduce_fusion = f32[512,2,128]{2,0,1:T(8,128)S(1)} fusion(f32[32,512,2,128]{3,1,2,0:T(8,128)} %all-to-all-done.1, f32[32,512,2]{1,2,0:T(2,128)S(1)} %get-tuple-element.22), kind=kLoop, calls=%fused_computation.6 | loop fusion | flops 8257536 | bytes 17432576 | tf_op jit(solution)/shard_map/reduce_sum | solution.py:106
  408.3 2.6 fusion.20
  410.9 2.5 convolution_convert_fusion
  413.4 1.6 convert_element_type.79
  416.2 1.9 fusion.29
  418.1 33.0 %reduce-scatter.2.cloned.1.call-done = bf16[512,256]{1,0:T(8,128)(2,1)} async-done(((bf16[512,1024]{1,0:T(8,128)(2,1)}), bf16[512,256]{1,0:T(8,128)(2,1)}) %reduce-scatter.2.cloned.1.call-update) | async-done | bytes 262160 | tf_op jit(solution)/shard_map/reduce_scatter | solution.py:142
  451.1 1.9 add_convert_fusion
  (110 shorter events, 29.3 us)
Async XLA Ops:
  7.2 20.4 %copy-start.1 = (bf16[512,1024]{1,0:T(8,128)(2,1)S(1)}, bf16[512,1024]{1,0:T(8,128)(2,1)}, u32[]{:S(2)}) copy-start(bf16[512,1024]{1,0:T(8,128)(2,1)} %param.9) | copy-start | bytes 3145732
  7.2 94.2 %all-gather.2.cloned.1.call-start = ((), (), s32[]{:S(2)}) async-start(), calls=%async_computation.4 | async-start | bytes 8650752 | tf_op jit(solution)/shard_map/all_gather | solution.py:91
  8.6 18.9 %collective-permute-start = (bf16[5,256,256]{1,2,0:T(8,128)(2,1)S(1)}, bf16[5,256,256]{1,2,0:T(8,128)(2,1)S(1)}, u32[]{:S(2)}, u32[]{:S(2)}) collective-permute-start(bf16[5,256,256]{1,2,0:T(8,128)(2,1)S(1)} %copy.54), channel_id=1, source_target_pairs={{0,4},{4,8},{8,12},{12,0},{1,5},{5,9},{9,13},{13,1},{2,6},{6,10},{... | collective-permute-start | bytes 1966088 | tf_op jit(solution)/shard_map/ppermute | solution.py:64
  10.7 17.2 %collective-permute-start.1 = (bf16[5,256,256]{1,2,0:T(8,128)(2,1)S(1)}, bf16[5,256,256]{1,2,0:T(8,128)(2,1)S(1)}, u32[]{:S(2)}, u32[]{:S(2)}) collective-permute-start(bf16[5,256,256]{1,2,0:T(8,128)(2,1)S(1)} %copy.54), channel_id=1, source_target_pairs={{0,12},{4,0},{8,4},{12,8},{1,13},{5,1},{9,5},{13,9},{2,14},{6,2},{... | collective-permute-start | bytes 1966088 | tf_op jit(solution)/shard_map/ppermute | solution.py:69
  13.3 31.4 %copy-start.24 = (f32[1024]{0:T(1024)S(1)}, f32[1024]{0:T(1024)}, u32[]{:S(2)}) copy-start(f32[1024]{0:T(1024)} %param.10) | copy-start | bytes 12292
  27.6 17.1 %collective-permute-start.2 = (bf16[5,256,256]{1,2,0:T(8,128)(2,1)S(1)}, bf16[5,256,256]{1,2,0:T(8,128)(2,1)S(1)}, u32[]{:S(2)}, u32[]{:S(2)}) collective-permute-start(bf16[5,256,256]{1,2,0:T(8,128)(2,1)S(1)} %collective-permute-done), channel_id=1, source_target_pairs={{0,4},{4,8},{8,12},{12,0},{1,5},{5,9},{9,13},{13,1},{2,6},{6,10},{... | collective-permute-start | bytes 1966088 | tf_op jit(solution)/shard_map/ppermute | solution.py:64
  44.8 2.3 copy-start.2
  47.1 1.4 copy-start.8
  49.4 21.0 %copy-start.23 = (s32[32]{0:T(128)S(1)}, s32[32]{0:T(128)}, u32[]{:S(2)}) copy-start(s32[32]{0:T(128)} %param.14) | copy-start | bytes 388
  119.3 21.6 %all-to-all-start = ((f32[32,512,2]{1,2,0:T(2,128)}), f32[32,512,2]{1,2,0:T(2,128)S(1)}, u32[]{:S(2)}, u32[]{:S(2)}) async-start(f32[32,512,2]{1,2,0:T(2,128)} %bitcast.10), calls=%async_computation | async-start | bytes 262144 | tf_op jit(solution)/shard_map/all_to_all | solution.py:100
  140.9 30.1 %all-to-all-start.2 = ((f32[32,512,2]{1,2,0:T(2,128)}), f32[32,512,2]{1,2,0:T(2,128)S(1)}, u32[]{:S(2)}, u32[]{:S(2)}) async-start(f32[32,512,2]{1,2,0:T(2,128)} %bitcast.14), calls=%async_computation.2 | async-start | bytes 262144 | tf_op jit(solution)/shard_map/all_to_all | solution.py:101
  171.0 7.6 %copy-start.11 = (bf16[2,16,256]{2,1,0:T(8,128)(2,1)S(1)}, bf16[2,16,256]{2,1,0:T(8,128)(2,1)}, u32[]{:S(2)}) copy-start(bf16[2,16,256]{2,1,0:T(8,128)(2,1)} %param.12) | copy-start | bytes 49156
  171.0 8.9 %copy-start.9 = (f32[1,8,2]{1,2,0:T(2,128)S(1)}, f32[1,8,2]{1,2,0:T(2,128)}, u32[]{:S(2)}) copy-start(f32[1,8,2]{1,2,0:T(2,128)} %param.17) | copy-start | bytes 196
  171.0 8.9 %copy-start.10 = (f32[1,8,2]{1,2,0:T(2,128)S(1)}, f32[1,8,2]{1,2,0:T(2,128)}, u32[]{:S(2)}) copy-start(f32[1,8,2]{1,2,0:T(2,128)} %param.16) | copy-start | bytes 196
  171.0 229.2 %all-to-all-start.1 = ((f32[32,512,2,128]{3,1,2,0:T(8,128)}), f32[32,512,2,128]{3,1,2,0:T(8,128)}, u32[]{:S(2)}, u32[]{:S(2)}) async-start(f32[32,512,2,128]{3,1,2,0:T(8,128)} %fusion.10), calls=%async_computation.1 | async-start | bytes 33554432 | tf_op jit(solution)/shard_map/all_to_all | solution.py:99
  178.5 272.6 %reduce-scatter.2.cloned.1.call-start = ((), (), s32[]{:S(2)}) async-start(), calls=%async_computation.5 | async-start | bytes 1310720 | tf_op jit(solution)/shard_map/reduce_scatter | solution.py:142
  179.9 3.5 copy-start.6
  182.6 3.3 copy-start.4
  182.6 9.4 %copy-start.21 = (f32[2]{0:T(128)S(1)}, f32[2]{0:T(128)}, u32[]{:S(2)}) copy-start(f32[2]{0:T(128)} %get-tuple-element.14) | copy-start | bytes 28
  182.6 9.4 %copy-start.22 = (f32[2]{0:T(128)S(1)}, f32[2]{0:T(128)}, u32[]{:S(2)}) copy-start(f32[2]{0:T(128)} %get-tuple-element.38) | copy-start | bytes 28
  183.1 12.6 %copy-start.19 = (f32[2]{0:T(128)S(1)}, f32[2]{0:T(128)}, u32[]{:S(2)}) copy-start(f32[2]{0:T(128)} %get-tuple-element.13) | copy-start | bytes 28
  183.1 12.6 %copy-start.20 = (f32[2]{0:T(128)S(1)}, f32[2]{0:T(128)}, u32[]{:S(2)}) copy-start(f32[2]{0:T(128)} %get-tuple-element.39) | copy-start | bytes 28
  183.3 3.8 copy-start.5
  184.4 15.5 %copy-start.17 = (f32[2]{0:T(128)S(1)}, f32[2]{0:T(128)}, u32[]{:S(2)}) copy-start(f32[2]{0:T(128)} %get-tuple-element.12) | copy-start | bytes 28
  184.4 15.5 %copy-start.18 = (f32[2]{0:T(128)S(1)}, f32[2]{0:T(128)}, u32[]{:S(2)}) copy-start(f32[2]{0:T(128)} %get-tuple-element.40) | copy-start | bytes 28
  184.6 1.4 copy-start
  184.9 19.3 %copy-start.15 = (f32[2]{0:T(128)S(1)}, f32[2]{0:T(128)}, u32[]{:S(2)}) copy-start(f32[2]{0:T(128)} %get-tuple-element.11) | copy-start | bytes 28
  184.9 19.3 %copy-start.16 = (f32[2]{0:T(128)S(1)}, f32[2]{0:T(128)}, u32[]{:S(2)}) copy-start(f32[2]{0:T(128)} %get-tuple-element.41) | copy-start | bytes 28
  188.3 20.1 %copy-start.14 = (f32[2]{0:T(128)S(1)}, f32[2]{0:T(128)}, u32[]{:S(2)}) copy-start(f32[2]{0:T(128)} %get-tuple-element.35) | copy-start | bytes 28
  190.7 20.9 %copy-start.7 = (f32[64,2,128]{0,2,1:T(8,128)S(1)}, f32[64,2,128]{0,2,1:T(8,128)}, u32[]{:S(2)}) copy-start(f32[64,2,128]{0,2,1:T(8,128)} %convolution_bitcast_fusion.9) | copy-start | bytes 196612
  400.2 8.1 %copy-start.12 = (bf16[16,2,128]{2,0,1:T(8,128)(2,1)S(1)}, bf16[16,2,128]{2,0,1:T(8,128)(2,1)}, u32[]{:S(2)}) copy-start(bf16[16,2,128]{2,0,1:T(8,128)(2,1)} %copy.57) | copy-start | bytes 24580
  413.4 2.8 copy-start.13
  (1 other events, 1.3 us)
Sparse Core Ops, SparseCore 0:
  49.5 51.7 all-gather.1
  413.5 37.4 reduce-scatter.1
